TPU v7x, 256 devices: a whole 4x4x8 slice. The times are simulated.
256 devices in a mesh: col: 32 (over z, x), row: 8 (over y, core).
Axes of the slice: x: 4, y: 4, z: 8, core: 2. Of those that a mesh axis runs over, the one named last changes fastest.
Arguments:
- trailing: float32 [24576, 16384], P('row', 'col'), may hold values from -6 to 6
- panel_rows: float32 [24576, 512], P(('row', 'col')), may hold values from -6 to 6
- pivot_block: float32 [512, 512], P('col'), as said below
- panel_fill: int32 [96, 2], replicated, may hold values 0 or 1
Outputs:
- updated: float32 [24576, 16384], P('row', 'col')
- panel_factor: float32 [24576, 512], P(('row', 'col'))
Inputs may be any that keep to these rules, and one draw needn't show every extreme that they name: `pivot_block`: Symmetric; each diagonal entry exceeds the sum of the magnitudes of the other entries of its row by at least 1. `panel_fill`: each entry is 1 with probability 0.15, independently of the others.
All inputs are finite; a program needn't handle non-finite values.
Results may differ from a plain program's by a relative error of at most 0.00008.
Values sent between devices are 32-bit elements; how exact they have to be, the bound alone decides.
A program may use at most 128 MiB of HBM per device.

v0:
```python
import jax
import jax.numpy as jnp
from jax import lax
from jax.sharding import PartitionSpec as P


def from_root(value, axis, source):
    kept = jnp.where(lax.axis_index(axis) == source, value, 0).astype(value.dtype)
    return lax.psum(kept, axis)


def apply_fill(values, row_start, fill_table, block_size):
    row_count = values.shape[0]
    blocks = (row_start + jnp.arange(row_count, dtype=jnp.int32)) // block_size
    one_hot = (blocks[:, None] == jnp.arange(fill_table.shape[0], dtype=jnp.int32)[None, :]).astype(
        jnp.float32
    )
    flags = jnp.dot(one_hot, fill_table.astype(jnp.float32), precision=lax.Precision.HIGHEST)
    shaped = values.reshape(row_count, 2, block_size) * flags[:, :, None]
    return shaped.reshape(row_count, 2 * block_size)


def solve_rows(values, factor):
    return lax.linalg.triangular_solve(
        factor, values, left_side=False, lower=True, transpose_a=True
    )


def per_device(trailing, panel_rows, pivot_block, panel_fill):
    block_size = panel_rows.shape[1] // 2
    piece_rows = panel_rows.shape[0]
    col_count = lax.axis_size("col")
    col_index = lax.axis_index("col")
    row_index = lax.axis_index("row")
    local_rows = piece_rows * col_count
    slab_start = row_index * local_rows
    pivot_full = lax.all_gather(pivot_block, "col", axis=0, tiled=True)
    factor = jnp.linalg.cholesky(pivot_full)
    piece_start = slab_start + col_index * piece_rows
    own_factor = solve_rows(apply_fill(panel_rows, piece_start, panel_fill, block_size), factor)
    row_side = lax.all_gather(own_factor, "col", axis=0, tiled=True)
    column_count = trailing.shape[1]
    column_start = col_index * column_count
    owner_row = column_start // local_rows
    offered = lax.dynamic_slice_in_dim(row_side, column_start - slab_start, column_count, 0)
    column_side = from_root(offered, "row", owner_row)
    update = lax.dot_general(
        row_side,
        column_side,
        (((1,), (1,)), ((), ())),
        precision=lax.Precision.HIGHEST,
        preferred_element_type=jnp.float32,
    )
    return (trailing - update, own_factor)


def solution(mesh):
    in_specs = (P("row", "col"), P(("row", "col"), None), P("col", None), P())
    out_specs = (P("row", "col"), P(("row", "col"), None))
    return jax.shard_map(
        per_device, mesh=mesh, in_specs=in_specs, out_specs=out_specs, check_vma=False
    )
```

profile of v0, /device:TPU:2, one launch (start us, length us, event | category | flops | bytes accessed | tf_op | source)
XLA Modules:
  0.0 402.2 jit_solution(7585898141999107908)
XLA Ops:
  7.2 0.7 all-gather.3.cloned.1.call-update
  8.0 0.9 fusion.28
  8.9 0.2 mul.22
  9.1 1.0 mul.24
  10.0 78.7 %all-gather.3.cloned.1.call-done = f32[512,512]{1,0:T(8,128)} async-done(((f32[16,512]{1,0:T(8,128)}), f32[512,512]{1,0:T(8,128)}) %all-gather.3.cloned.1.call-update) | async-done | bytes 1048592 | tf_op jit(solution)/shard_map/all_gather | solution.py:37
  88.7 1.6 copy.10
  90.3 1.4 fusion
  91.8 11.7 %cholesky.104 = f32[128,128]{1,0:T(8,128)S(1)} custom-call(f32[128,128]{1,0:T(8,128)S(1)} %cholesky.266), custom_call_target="Cholesky" | custom-call | tf_op jit(solution)/shard_map/jit(cholesky)/cholesky | solution.py:38
  103.5 9.8 %custom-call.30 = f32[1,128,128]{1,2,0:T(8,128)S(1)} custom-call(f32[1,128,128]{2,1,0:T(8,128)S(1)} %get-tuple-element.29), custom_call_target="InvertDiagBlocksLowerTriangular" | custom-call | tf_op jit(solution)/shard_map/jit(cholesky)/cholesky | solution.py:38
  113.3 0.1 cholesky.224
  113.5 0.3 constant_dynamic-update-slice_fusion.3
  113.8 0.3 convolution_subtract_fusion.1
  114.1 11.7 %cholesky.217 = f32[128,128]{1,0:T(8,128)S(1)} custom-call(f32[128,128]{1,0:T(8,128)S(1)} %cholesky.270), custom_call_target="Cholesky" | custom-call | tf_op jit(solution)/shard_map/jit(cholesky)/cholesky | solution.py:38
  125.9 10.0 %custom-call.31 = f32[1,128,128]{1,2,0:T(8,128)S(1)} custom-call(f32[1,128,128]{2,1,0:T(8,128)S(1)} %get-tuple-element.26), custom_call_target="InvertDiagBlocksLowerTriangular" | custom-call | tf_op jit(solution)/shard_map/jit(cholesky)/cholesky | solution.py:38
  135.8 0.3 convolution_dynamic-update-slice_fusion
  136.1 0.4 convolution_subtract_fusion.2
  136.5 11.7 %cholesky.238 = f32[128,128]{1,0:T(8,128)S(1)} custom-call(f32[128,128]{1,0:T(8,128)S(1)} %cholesky.275), custom_call_target="Cholesky" | custom-call | tf_op jit(solution)/shard_map/jit(cholesky)/cholesky | solution.py:38
  148.3 0.7 compare_reduce_fusion.1
  149.0 9.8 %custom-call.32 = f32[1,128,128]{1,2,0:T(8,128)S(1)} custom-call(f32[1,128,128]{2,1,0:T(8,128)S(1)} %get-tuple-element.23), custom_call_target="InvertDiagBlocksLowerTriangular" | custom-call | tf_op jit(solution)/shard_map/jit(cholesky)/cholesky | solution.py:38
  158.8 0.2 convolution_dynamic-update-slice_fusion.1
  159.0 0.4 convolution_subtract_fusion.3
  159.4 11.9 %cholesky.255 = f32[128,128]{1,0:T(8,128)S(1)} custom-call(f32[128,128]{1,0:T(8,128)S(1)} %convolution_subtract_fusion.3), custom_call_target="Cholesky" | custom-call | tf_op jit(solution)/shard_map/jit(cholesky)/cholesky | solution.py:38
  171.3 0.6 compare_reduce_fusion
  171.9 0.7 compare_reduce_fusion.2
  175.1 0.1 select_select_fusion
  175.3 8.5 %while.1 = (s32[]{:T(128)}, f32[512,512]{1,0:T(8,128)S(1)}, s32[4,2]{0,1:T(2,128)S(1)}, f32[4,128,128]{2,1,0:T(8,128)S(1)}, s32[]{:T(128)}) while((s32[]{:T(128)}, f32[512,512]{1,0:T(8,128)S(1)}, s32[4,2]{0,1:T(2,128)S(1)}, f32[4,128,128]{2,1,0:T(8,128)S(1)}, s32[]{:T(128)}) %tuple.31), condition=%wide.while_cond, body=%wide.while_body.sunk | while | flops 2 | bytes 131189 | solution.py:24
  175.4 0.6 fusion.42
  176.0 1.4 bitcast_dynamic-update-slice_fusion.2
  177.5 0.6 fusion.42
  178.1 1.4 bitcast_dynamic-update-slice_fusion.2
  179.5 0.1 constant_dynamic-slice_fusion.2
  179.6 0.6 fusion.42
  180.2 1.4 bitcast_dynamic-update-slice_fusion.2
  181.7 0.6 fusion.42
  182.3 1.4 bitcast_dynamic-update-slice_fusion.2
  183.8 39.3 %custom-call.33 = f32[4,128,128]{1,2,0:T(8,128)S(1)} custom-call(f32[4,128,128]{2,1,0:T(8,128)S(1)} %get-tuple-element.9), custom_call_target="InvertDiagBlocksLowerTriangular" | custom-call | tf_op jit(solution)/shard_map/triangular_solve | solution.py:24
  223.1 0.2 fusion.21
  223.3 0.2 convolution_subtract_fusion.5
  223.6 0.2 fusion.19
  223.8 0.3 convolution_subtract_fusion.4
  224.0 0.2 fusion.18
  224.2 0.4 convolution_subtract_fusion.6
  224.6 0.2 fusion.17
  224.8 0.7 pad_maximum_fusion
  225.6 86.1 %all-gather.5.cloned.1.call-done = f32[3072,512]{1,0:T(8,128)} async-done(((f32[96,512]{1,0:T(8,128)}), f32[3072,512]{1,0:T(8,128)}) %all-gather.5.cloned.1.call-update) | async-done | bytes 6291472 | tf_op jit(solution)/shard_map/all_gather | solution.py:41
  311.8 2.3 dynamic-slice_select_fusion
  314.1 66.5 %all-reduce.3.cloned.1.call-done = f32[512,512]{1,0:T(8,128)} async-done(((f32[512,512]{1,0:T(8,128)}), f32[512,512]{1,0:T(8,128)}) %all-reduce.3.cloned.1.call-update) | async-done | bytes 1048592 | tf_op jit(solution)/shard_map/psum | solution.py:9
  380.5 15.1 %convolution_subtract_fusion = f32[3072,512]{1,0:T(8,128)} fusion(f32[3072,512]{1,0:T(8,128)} %param.4, f32[3072,512]{1,0:T(8,128)} %all-gather.5.cloned.1.call-done, f32[512,512]{1,0:T(8,128)} %all-reduce.3.cloned.1.call-done), kind=kOutput, calls=%fused_computation.2 | convolution fusion | flops 9665249280 | bytes 19922944 | tf_op jit(solution)/shard_map/dot_general | solution.py:47
  (20 shorter events, 0.6 us)
Async XLA Ops:
  7.2 81.6 %all-gather.3.cloned.1.call-start = ((), (), s32[]{:S(2)}) async-start(), calls=%async_computation | async-start | bytes 1081344 | tf_op jit(solution)/shard_map/all_gather | solution.py:37
  7.9 303.9 %all-gather.5.cloned.1.call-start = ((), (), s32[]{:S(2)}) async-start(), calls=%async_computation.1 | async-start | bytes 6488064 | tf_op jit(solution)/shard_map/all_gather | solution.py:41
  225.5 155.0 %all-reduce.3.cloned.1.call-start = ((), (), s32[]{:S(2)}) async-start(), calls=%async_computation.2 | async-start | bytes 2097152 | tf_op jit(solution)/shard_map/psum | solution.py:9
Sparse Core Ops, SparseCore 0:
  10.6 78.1 all-gather.2
  225.7 86.0 all-gather.4
  314.7 65.7 all-reduce.2
where the time goes:
time: 403 us; the launch traced here: 402 us
  waiting for transfers between devices  232 us (58%)
  other arithmetic  124 us (31%)
  matrix products  19.6 us (5%)
  between operations  16.6 us (4%)
  local copies, waits for them, and re-layouts  10.3 us (3%)
    all_gather x1, waiting for transfers between devices, per_device(): row_side = lax.all_gather(own_factor, 'col', axis=0, tiled=True)  86.1 us
    another operation x14, other arithmetic, per_device(): factor = jnp.linalg.cholesky(pivot_full)  78.7 us
    all_gather x1, waiting for transfers between devices, per_device(): pivot_full = lax.all_gather(pivot_block, 'col', axis=0, tiled=True)  78.7 us
    psum x1, waiting for transfers between devices, from_root(): return lax.psum(kept, axis)  66.5 us
    another operation x4, other arithmetic, solve_rows(): lax.linalg.triangular_solve(factor, values, left_side=False, lower=True,...  40.1 us
    dot_general x1, matrix products, per_device(): lax.dot_general(row_side, column_side, (((1,), (1,)), ((), ())), precisio...  15.1 us
    another operation x12, local copies, waits for them, and re-layouts  8.39 us
  transfers between devices with their start and end apart: 3, of which 3 were waited for; matrix products, arithmetic and copies ran while one was open for 1% of the time, Pallas kernels for 0%

commit v1 on v0

--- a/solution.py
+++ b/solution.py
@@ -34,7 +34,8 @@
     row_index = lax.axis_index("row")
     local_rows = piece_rows * col_count
     slab_start = row_index * local_rows
-    pivot_full = lax.all_gather(pivot_block, "col", axis=0, tiled=True)
+    sent = jnp.stack([pivot_block] * lax.axis_size("col"))
+    pivot_full = jnp.concatenate(lax.all_to_all(sent, "col", 0, 0), axis=0)
     factor = jnp.linalg.cholesky(pivot_full)
     piece_start = slab_start + col_index * piece_rows
     own_factor = solve_rows(apply_fill(panel_rows, piece_start, panel_fill, block_size), factor)

time: 403 us -> 362 us (0.90)
  waiting for transfers between devices: 232 us -> 177 us
  starting transfers between devices: 0.12 us -> 11.7 us
    all_gather x1 -> x0, waiting for transfers between devices: 78.7 us -> none  [per_device(): pivot_full = lax.all_gather(pivot_block, 'col', axis=0, tiled=True)]
    all_to_all x0 -> x1, waiting for transfers between devices: none -> 25.9 us  [per_device(): pivot_full = jnp.concatenate(lax.all_to_all(sent, 'col', 0, 0), axis=0)]
    all_to_all x0 -> x1, starting transfers between devices: none -> 11.6 us  [per_device(): pivot_full = jnp.concatenate(lax.all_to_all(sent, 'col', 0, 0), axis=0)]
    another operation x12 -> x13, local copies, waits for them, and re-layouts: 8.39 us -> 12.4 us
where the time goes in v1:
time: 362 us; the launch traced here: 361 us
  waiting for transfers between devices  177 us (49%)
  other arithmetic  123 us (34%)
  matrix products  19.6 us (5%)
  between operations  16.8 us (5%)
  local copies, waits for them, and re-layouts  13 us (4%)
  starting transfers between devices  11.7 us (3%)
    all_gather x1, waiting for transfers between devices, per_device(): row_side = lax.all_gather(own_factor, 'col', axis=0, tiled=True)  84.4 us
    another operation x14, other arithmetic, per_device(): factor = jnp.linalg.cholesky(pivot_full)  78.8 us
    psum x1, waiting for transfers between devices, from_root(): return lax.psum(kept, axis)  66.5 us
    another operation x4, other arithmetic, solve_rows(): lax.linalg.triangular_solve(factor, values, left_side=False, lower=True,...  40.9 us
    all_to_all x1, waiting for transfers between devices, per_device(): pivot_full = jnp.concatenate(lax.all_to_all(sent, 'col', 0, 0), axis=0)  25.9 us
    dot_general x1, matrix products, per_device(): lax.dot_general(row_side, column_side, (((1,), (1,)), ((), ())), precisio...  15.1 us
    all_to_all x1, starting transfers between devices, per_device(): pivot_full = jnp.concatenate(lax.all_to_all(sent, 'col', 0, 0), axis=0)  11.6 us
    another operation x12, local copies, waits for them, and re-layouts  10.5 us
  transfers between devices with their start and end apart: 3, of which 3 were waited for; matrix products, arithmetic and copies ran while one was open for 1% of the time, Pallas kernels for 0%

profile of v1, /device:TPU:2, one launch (start us, length us, event | category | flops | bytes accessed | tf_op | source)
XLA Modules:
  0.0 361.1 jit_solution(8854732701757599269)
XLA Ops:
  7.2 1.9 stack.2
  9.0 11.6 %all-to-all-start = ((f32[32,16,512]{2,1,0:T(8,128)}), f32[32,16,512]{2,1,0:T(8,128)S(1)}, u32[]{:S(2)}, u32[]{:S(2)}) async-start(f32[32,16,512]{2,1,0:T(8,128)} %stack.2), calls=%async_computation | async-start | bytes 2097152 | tf_op jit(solution)/shard_map/all_to_all | solution.py:38
  20.7 0.9 fusion.28
  21.6 0.2 mul.22
  21.8 1.0 mul.24
  22.8 25.9 %all-to-all-done = f32[32,16,512]{2,1,0:T(8,128)S(1)} async-done(((f32[32,16,512]{2,1,0:T(8,128)}), f32[32,16,512]{2,1,0:T(8,128)S(1)}, u32[]{:S(2)}, u32[]{:S(2)}) %all-to-all-start) | async-done | bytes 1048608 | tf_op jit(solution)/shard_map/all_to_all | solution.py:38
  48.7 0.3 copy.10
  49.0 0.2 fusion
  49.3 11.7 %cholesky.104 = f32[128,128]{1,0:T(8,128)S(1)} custom-call(f32[128,128]{1,0:T(8,128)S(1)} %cholesky.266), custom_call_target="Cholesky" | custom-call | tf_op jit(solution)/shard_map/jit(cholesky)/cholesky | solution.py:39
  61.1 9.8 %custom-call.30 = f32[1,128,128]{1,2,0:T(8,128)S(1)} custom-call(f32[1,128,128]{2,1,0:T(8,128)S(1)} %get-tuple-element.29), custom_call_target="InvertDiagBlocksLowerTriangular" | custom-call | tf_op jit(solution)/shard_map/jit(cholesky)/cholesky | solution.py:39
  71.0 0.3 constant_dynamic-update-slice_fusion.3
  71.3 0.3 convolution_subtract_fusion.1
  71.7 11.7 %cholesky.217 = f32[128,128]{1,0:T(8,128)S(1)} custom-call(f32[128,128]{1,0:T(8,128)S(1)} %cholesky.270), custom_call_target="Cholesky" | custom-call | tf_op jit(solution)/shard_map/jit(cholesky)/cholesky | solution.py:39
  83.4 9.9 %custom-call.31 = f32[1,128,128]{1,2,0:T(8,128)S(1)} custom-call(f32[1,128,128]{2,1,0:T(8,128)S(1)} %get-tuple-element.26), custom_call_target="InvertDiagBlocksLowerTriangular" | custom-call | tf_op jit(solution)/shard_map/jit(cholesky)/cholesky | solution.py:39
  93.4 0.3 convolution_dynamic-update-slice_fusion
  93.6 0.4 convolution_subtract_fusion.2
  94.0 11.7 %cholesky.238 = f32[128,128]{1,0:T(8,128)S(1)} custom-call(f32[128,128]{1,0:T(8,128)S(1)} %cholesky.275), custom_call_target="Cholesky" | custom-call | tf_op jit(solution)/shard_map/jit(cholesky)/cholesky | solution.py:39
  105.8 0.7 compare_reduce_fusion.1
  106.5 9.8 %custom-call.32 = f32[1,128,128]{1,2,0:T(8,128)S(1)} custom-call(f32[1,128,128]{2,1,0:T(8,128)S(1)} %get-tuple-element.23), custom_call_target="InvertDiagBlocksLowerTriangular" | custom-call | tf_op jit(solution)/shard_map/jit(cholesky)/cholesky | solution.py:39
  116.3 0.2 convolution_dynamic-update-slice_fusion.1
  116.5 0.4 convolution_subtract_fusion.3
  116.9 11.7 %cholesky.255 = f32[128,128]{1,0:T(8,128)S(1)} custom-call(f32[128,128]{1,0:T(8,128)S(1)} %convolution_subtract_fusion.3), custom_call_target="Cholesky" | custom-call | tf_op jit(solution)/shard_map/jit(cholesky)/cholesky | solution.py:39
  128.6 0.3 select_reduce_fusion
  128.9 0.7 compare_reduce_fusion
  129.5 0.6 compare_reduce_fusion.2
  132.6 0.1 select_select_fusion
  132.8 10.5 %while.1 = (s32[]{:T(128)}, f32[512,512]{1,0:T(8,128)S(1)}, s32[4,2]{0,1:T(2,128)S(1)}, f32[4,128,128]{2,1,0:T(8,128)}, s32[]{:T(128)}) while((s32[]{:T(128)}, f32[512,512]{1,0:T(8,128)S(1)}, s32[4,2]{0,1:T(2,128)S(1)}, f32[4,128,128]{2,1,0:T(8,128)}, s32[]{:T(128)}) %tuple.31), condition=%wide.while_cond, body=%wide.while_body.sunk | while | flops 2 | bytes 132205 | solution.py:24
  132.9 0.6 fusion.42
  133.4 2.0 bitcast_dynamic-update-slice_fusion.2
  135.5 0.6 fusion.42
  136.1 2.0 bitcast_dynamic-update-slice_fusion.2
  138.1 0.6 fusion.42
  138.7 2.0 bitcast_dynamic-update-slice_fusion.2
  140.7 0.6 fusion.42
  141.3 2.0 bitcast_dynamic-update-slice_fusion.2
  143.3 40.1 %custom-call.33 = f32[4,128,128]{1,2,0:T(8,128)S(1)} custom-call(f32[4,128,128]{2,1,0:T(8,128)} %get-tuple-element.9), custom_call_target="InvertDiagBlocksLowerTriangular" | custom-call | tf_op jit(solution)/shard_map/triangular_solve | solution.py:24
  183.4 0.2 fusion.21
  183.6 0.2 convolution_subtract_fusion.5
  183.9 0.2 fusion.19
  184.1 0.3 convolution_subtract_fusion.4
  184.4 0.2 fusion.18
  184.6 0.4 convolution_subtract_fusion.6
  185.0 0.2 fusion.17
  185.2 0.7 pad_maximum_fusion
  186.0 84.4 %all-gather.2.cloned.1.call-done = f32[3072,512]{1,0:T(8,128)} async-done(((f32[96,512]{1,0:T(8,128)}), f32[3072,512]{1,0:T(8,128)}) %all-gather.2.cloned.1.call-update) | async-done | bytes 6291472 | tf_op jit(solution)/shard_map/all_gather | solution.py:42
  270.4 2.3 dynamic-slice_select_fusion
  272.7 66.5 %all-reduce.3.cloned.1.call-done = f32[512,512]{1,0:T(8,128)} async-done(((f32[512,512]{1,0:T(8,128)}), f32[512,512]{1,0:T(8,128)}) %all-reduce.3.cloned.1.call-update) | async-done | bytes 1048592 | tf_op jit(solution)/shard_map/psum | solution.py:9
  339.2 15.1 %convolution_subtract_fusion = f32[3072,512]{1,0:T(8,128)} fusion(f32[3072,512]{1,0:T(8,128)} %param.4, f32[3072,512]{1,0:T(8,128)} %all-gather.2.cloned.1.call-done, f32[512,512]{1,0:T(8,128)} %all-reduce.3.cloned.1.call-done), kind=kOutput, calls=%fused_computation.2 | convolution fusion | flops 9665249280 | bytes 19922944 | tf_op jit(solution)/shard_map/dot_general | solution.py:48
  (20 shorter events, 0.7 us)
Async XLA Ops:
  9.0 39.7 %all-to-all-start = ((f32[32,16,512]{2,1,0:T(8,128)}), f32[32,16,512]{2,1,0:T(8,128)S(1)}, u32[]{:S(2)}, u32[]{:S(2)}) async-start(f32[32,16,512]{2,1,0:T(8,128)} %stack.2), calls=%async_computation | async-start | bytes 2097152 | tf_op jit(solution)/shard_map/all_to_all | solution.py:38
  20.6 249.8 %all-gather.2.cloned.1.call-start = ((), (), s32[]{:S(2)}) async-start(), calls=%async_computation.1 | async-start | bytes 6488064 | tf_op jit(solution)/shard_map/all_gather | solution.py:42
  185.9 153.3 %all-reduce.3.cloned.1.call-start = ((), (), s32[]{:S(2)}) async-start(), calls=%async_computation.2 | async-start | bytes 2097152 | tf_op jit(solution)/shard_map/psum | solution.py:9
Sparse Core Ops, SparseCore 0:
  186.0 84.3 all-gather.1
  273.3 65.7 all-reduce.2

commit v2 on v0

--- a/solution.py
+++ b/solution.py
@@ -4,9 +4,15 @@
 from jax.sharding import PartitionSpec as P
 
 
+def gather_and_add(x, axis):
+    shards = lax.all_gather(x, axis, axis=0, tiled=False)
+    total = shards.sum(axis=0)
+    return total
+
+
 def from_root(value, axis, source):
     kept = jnp.where(lax.axis_index(axis) == source, value, 0).astype(value.dtype)
-    return lax.psum(kept, axis)
+    return gather_and_add(kept, axis)
 
 
 def apply_fill(values, row_start, fill_table, block_size):

time: 403 us -> 392 us (0.973)
  waiting for transfers between devices: 232 us -> 216 us
    psum x1 -> x0, waiting for transfers between devices: 66.5 us -> none  [from_root(): return lax.psum(kept, axis)]
    all_gather x0 -> x1, waiting for transfers between devices: none -> 50.7 us  [gather_and_add(): shards = lax.all_gather(x, axis, axis=0, tiled=False)]
    reduce_sum x0 -> x1, other arithmetic: none -> 4.49 us  [gather_and_add(): total = shards.sum(axis=0)]
where the time goes in v2:
time: 392 us; the launch traced here: 391 us
  waiting for transfers between devices  216 us (55%)
  other arithmetic  128 us (33%)
  matrix products  19.4 us (5%)
  between operations  16.6 us (4%)
  local copies, waits for them, and re-layouts  10.3 us (3%)
    all_gather x1, waiting for transfers between devices, per_device(): row_side = lax.all_gather(own_factor, 'col', axis=0, tiled=True)  86.1 us
    another operation x14, other arithmetic, per_device(): factor = jnp.linalg.cholesky(pivot_full)  78.7 us
    all_gather x1, waiting for transfers between devices, per_device(): pivot_full = lax.all_gather(pivot_block, 'col', axis=0, tiled=True)  78.7 us
    all_gather x1, waiting for transfers between devices, gather_and_add(): shards = lax.all_gather(x, axis, axis=0, tiled=False)  50.7 us
    another operation x4, other arithmetic, solve_rows(): lax.linalg.triangular_solve(factor, values, left_side=False, lower=True,...  40.1 us
    dot_general x1, matrix products, per_device(): lax.dot_general(row_side, column_side, (((1,), (1,)), ((), ())), precisio...  14.9 us
    another operation x12, local copies, waits for them, and re-layouts  8.39 us
  transfers between devices with their start and end apart: 3, of which 3 were waited for; matrix products, arithmetic and copies ran while one was open for 1% of the time, Pallas kernels for 0%

profile of v2, /device:TPU:2, one launch (start us, length us, event | category | flops | bytes accessed | tf_op | source)
XLA Modules:
  0.0 390.7 jit_solution(17263039285143425229)
XLA Ops:
  7.2 0.7 all-gather.5.cloned.1.call-update
  8.0 0.9 fusion.28
  8.9 0.2 mul.22
  9.1 1.0 mul.24
  10.0 78.7 %all-gather.5.cloned.1.call-done = f32[512,512]{1,0:T(8,128)} async-done(((f32[16,512]{1,0:T(8,128)}), f32[512,512]{1,0:T(8,128)}) %all-gather.5.cloned.1.call-update) | async-done | bytes 1048592 | tf_op jit(solution)/shard_map/all_gather | solution.py:43
  88.7 1.6 copy.10
  90.3 1.4 fusion
  91.8 11.7 %cholesky.104 = f32[128,128]{1,0:T(8,128)S(1)} custom-call(f32[128,128]{1,0:T(8,128)S(1)} %cholesky.266), custom_call_target="Cholesky" | custom-call | tf_op jit(solution)/shard_map/jit(cholesky)/cholesky | solution.py:44
  103.5 9.8 %custom-call.30 = f32[1,128,128]{1,2,0:T(8,128)S(1)} custom-call(f32[1,128,128]{2,1,0:T(8,128)S(1)} %get-tuple-element.29), custom_call_target="InvertDiagBlocksLowerTriangular" | custom-call | tf_op jit(solution)/shard_map/jit(cholesky)/cholesky | solution.py:44
  113.3 0.1 cholesky.224
  113.5 0.3 constant_dynamic-update-slice_fusion.3
  113.8 0.3 convolution_subtract_fusion.1
  114.1 11.7 %cholesky.217 = f32[128,128]{1,0:T(8,128)S(1)} custom-call(f32[128,128]{1,0:T(8,128)S(1)} %cholesky.270), custom_call_target="Cholesky" | custom-call | tf_op jit(solution)/shard_map/jit(cholesky)/cholesky | solution.py:44
  125.9 10.0 %custom-call.31 = f32[1,128,128]{1,2,0:T(8,128)S(1)} custom-call(f32[1,128,128]{2,1,0:T(8,128)S(1)} %get-tuple-element.26), custom_call_target="InvertDiagBlocksLowerTriangular" | custom-call | tf_op jit(solution)/shard_map/jit(cholesky)/cholesky | solution.py:44
  135.8 0.3 convolution_dynamic-update-slice_fusion
  136.1 0.4 convolution_subtract_fusion.2
  136.5 11.7 %cholesky.238 = f32[128,128]{1,0:T(8,128)S(1)} custom-call(f32[128,128]{1,0:T(8,128)S(1)} %cholesky.275), custom_call_target="Cholesky" | custom-call | tf_op jit(solution)/shard_map/jit(cholesky)/cholesky | solution.py:44
  148.3 0.7 compare_reduce_fusion.1
  149.0 9.8 %custom-call.32 = f32[1,128,128]{1,2,0:T(8,128)S(1)} custom-call(f32[1,128,128]{2,1,0:T(8,128)S(1)} %get-tuple-element.23), custom_call_target="InvertDiagBlocksLowerTriangular" | custom-call | tf_op jit(solution)/shard_map/jit(cholesky)/cholesky | solution.py:44
  158.8 0.2 convolution_dynamic-update-slice_fusion.1
  159.0 0.4 convolution_subtract_fusion.3
  159.4 11.9 %cholesky.255 = f32[128,128]{1,0:T(8,128)S(1)} custom-call(f32[128,128]{1,0:T(8,128)S(1)} %convolution_subtract_fusion.3), custom_call_target="Cholesky" | custom-call | tf_op jit(solution)/shard_map/jit(cholesky)/cholesky | solution.py:44
  171.3 0.6 compare_reduce_fusion
  171.9 0.7 compare_reduce_fusion.2
  175.1 0.1 select_select_fusion
  175.3 8.5 %while.1 = (s32[]{:T(128)}, f32[512,512]{1,0:T(8,128)S(1)}, s32[4,2]{0,1:T(2,128)S(1)}, f32[4,128,128]{2,1,0:T(8,128)S(1)}, s32[]{:T(128)}) while((s32[]{:T(128)}, f32[512,512]{1,0:T(8,128)S(1)}, s32[4,2]{0,1:T(2,128)S(1)}, f32[4,128,128]{2,1,0:T(8,128)S(1)}, s32[]{:T(128)}) %tuple.31), condition=%wide.while_cond, body=%wide.while_body.sunk | while | flops 2 | bytes 131189 | solution.py:30
  175.4 0.6 fusion.42
  176.0 1.4 bitcast_dynamic-update-slice_fusion.2
  177.5 0.6 fusion.42
  178.1 1.4 bitcast_dynamic-update-slice_fusion.2
  179.6 0.6 fusion.42
  180.2 1.4 bitcast_dynamic-update-slice_fusion.2
  181.7 0.6 fusion.42
  182.3 1.4 bitcast_dynamic-update-slice_fusion.2
  183.8 39.3 %custom-call.33 = f32[4,128,128]{1,2,0:T(8,128)S(1)} custom-call(f32[4,128,128]{2,1,0:T(8,128)S(1)} %get-tuple-element.9), custom_call_target="InvertDiagBlocksLowerTriangular" | custom-call | tf_op jit(solution)/shard_map/triangular_solve | solution.py:30
  223.1 0.2 fusion.21
  223.3 0.2 convolution_subtract_fusion.5
  223.6 0.2 fusion.19
  223.8 0.3 convolution_subtract_fusion.4
  224.0 0.2 fusion.18
  224.2 0.4 convolution_subtract_fusion.6
  224.6 0.2 fusion.17
  224.8 0.7 pad_maximum_fusion
  225.6 86.1 %all-gather.7.cloned.1.call-done = f32[3072,512]{1,0:T(8,128)} async-done(((f32[96,512]{1,0:T(8,128)}), f32[3072,512]{1,0:T(8,128)}) %all-gather.7.cloned.1.call-update) | async-done | bytes 6291472 | tf_op jit(solution)/shard_map/all_gather | solution.py:47
  311.8 2.3 dynamic-slice_select_fusion
  314.1 50.7 %all-gather.9.cloned.1.call-done = f32[4096,512]{1,0:T(8,128)} async-done(((f32[512,512]{1,0:T(8,128)}), f32[4096,512]{1,0:T(8,128)}) %all-gather.9.cloned.1.call-update) | async-done | bytes 8388624 | tf_op jit(solution)/shard_map/all_gather | solution.py:8
  364.7 4.5 %reduce_sum.9 = f32[512,512]{1,0:T(8,128)S(1)} reduce(f32[8,512,512]{2,1,0:T(8,128)} %bitcast.53, f32[]{:T(128)} %constant.175.clone.1), dimensions={0}, to_apply=%region_8.9 | reduce | flops 1835008 | bytes 9437188 | tf_op jit(solution)/shard_map/reduce_sum | solution.py:9
  369.2 14.9 %convolution_subtract_fusion = f32[3072,512]{1,0:T(8,128)} fusion(f32[3072,512]{1,0:T(8,128)} %param.4, f32[3072,512]{1,0:T(8,128)} %all-gather.7.cloned.1.call-done, f32[512,512]{1,0:T(8,128)S(1)} %reduce_sum.9), kind=kOutput, calls=%fused_computation.2 | convolution fusion | flops 9665249280 | bytes 19922944 | tf_op jit(solution)/shard_map/dot_general | solution.py:53
  (21 shorter events, 0.6 us)
Async XLA Ops:
  7.2 81.6 %all-gather.5.cloned.1.call-start = ((), (), s32[]{:S(2)}) async-start(), calls=%async_computation | async-start | bytes 1081344 | tf_op jit(solution)/shard_map/all_gather | solution.py:43
  7.9 303.9 %all-gather.7.cloned.1.call-start = ((), (), s32[]{:S(2)}) async-start(), calls=%async_computation.1 | async-start | bytes 6488064 | tf_op jit(solution)/shard_map/all_gather | solution.py:47
  225.5 139.2 %all-gather.9.cloned.1.call-start = ((), (), s32[]{:S(2)}) async-start(), calls=%async_computation.2 | async-start | bytes 9437184 | tf_op jit(solution)/shard_map/all_gather | solution.py:8
Sparse Core Ops, SparseCore 0:
  10.6 78.1 all-gather.4
  225.7 86.0 all-gather.6
  314.2 50.4 all-gather.8
